TPU v7x, 32 devices: a whole 2x2x4 slice. The times are simulated.
32 devices in a mesh: parts: 2 (over y), dp: 4 (over z), tensor: 4 (over x, core).
Axes of the slice: x: 2, y: 2, z: 4, core: 2. Of those that a mesh axis runs over, the one named last changes fastest.
Arguments:
- prompt_kv: bfloat16 [2, 14336, 8, 128], P(None, ('parts', 'dp'), 'tensor'), parts along dimension 1, may hold values from -12 to 12
- gen_kv: bfloat16 [64, 2, 128, 8, 128], P(('parts', 'dp'), None, None, 'tensor'), parts along dimension 0, may hold values from -17 to 17
- queries: bfloat16 [2, 64, 64, 128], P(None, ('parts', 'dp'), 'tensor'), parts along dimension 1, may hold values from -24 to 24
- new_kv: bfloat16 [2, 2, 64, 8, 128], P(None, None, ('parts', 'dp'), 'tensor'), parts along dimension 2, may hold values from -48 to 48
- ancestors: int32 [64], P(('parts', 'dp')), parts along dimension 0, may hold values from 0 to 31, as said below
- prior_twist: float32 [64], P(('parts', 'dp')), parts along dimension 0, may hold values from -290 to 6
- twist_vec: float32 [64, 128], P('tensor'), may hold values from -1 to 1
Outputs:
- attended: bfloat16 [2, 64, 64, 128], P(None, ('parts', 'dp'), 'tensor'), parts along dimension 1
- log_weights: float32 [64], P(('parts', 'dp')), parts along dimension 0
There are 2 independent parts, one for each index of `parts`. A program takes and returns all parts, laid end to end along the dimension named above; an argument that names none is the same for every part. Nothing has to cross between parts.
Inputs may be any that keep to these rules, and one draw needn't show every extreme that they name: Duplicates are allowed. Among the 8 particles of one device (equal p // 8) at most 4 have ancestors held by one same device (equal ancestors // 8), and every device has exactly 4 from some device.
All inputs are finite; a program needn't handle non-finite values.
Results may differ from a plain program's by a relative error of at most 0.0017.
Values may be sent and summed in bfloat16 or wider, within the bound.
A program may use at most 128 MiB of HBM per device.

v0:
```python
import math
import jax
import jax.numpy as jnp
from jax import lax
from jax.sharding import PartitionSpec as P


def join_states(left_state, right_state):
    largest = jnp.maximum(left_state[0], right_state[0])
    left_scale = jnp.exp(left_state[0] - largest)
    right_scale = jnp.exp(right_state[0] - largest)
    return (
        largest,
        left_state[1] * left_scale + right_state[1] * right_scale,
        left_state[2] * left_scale[..., None] + right_state[2] * right_scale[..., None],
    )


def fold_blocks(moments, totals, weighted, along):
    largest = jnp.max(moments, axis=along)
    scale_each = jnp.exp(moments - jnp.expand_dims(largest, along))
    return (
        largest,
        jnp.sum(totals * scale_each, axis=along),
        jnp.sum(weighted * scale_each[..., None], axis=along),
    )


def block_state(scores, values, pattern):
    largest = jnp.max(scores, axis=-1)
    exponent = jnp.exp(scores - largest[..., None])
    weighted = jnp.einsum(
        pattern, exponent.astype(jnp.bfloat16), values, preferred_element_type=jnp.float32
    )
    return (largest, jnp.sum(exponent, axis=-1), weighted)


def prompt_states(query_rows, prompt_kv, kv_count, scaling):
    row_count, head_count, head_size = query_rows.shape
    group_size = head_count // kv_count
    per_block = math.gcd(row_count, 256)
    blocked = query_rows.reshape(row_count // per_block, per_block, kv_count, group_size, head_size)
    key_rows = prompt_kv[0]
    values = prompt_kv[1]

    def attend_block(query_block):
        scores = (
            jnp.einsum("pcgd,kcd->pcgk", query_block, key_rows, preferred_element_type=jnp.float32)
            * scaling
        )
        return block_state(scores, values, "pcgk,kcd->pcgd")

    largest, totals, weighted = lax.map(attend_block, blocked)
    return (
        largest.reshape(row_count, head_count),
        totals.reshape(row_count, head_count),
        weighted.reshape(row_count, head_count, head_size),
    )


def per_device(prompt_kv, gen_kv, queries, new_kv, ancestors, prior_twist, twist_vec):
    step_count, local_count, head_count, head_size = queries.shape
    kv_count = prompt_kv.shape[2]
    group_size = head_count // kv_count
    scaling = 1.0 / math.sqrt(head_size)
    devices = lax.axis_size("dp")
    capacity = max(2, (2 * local_count + devices - 1) // devices)
    slot_total = devices * capacity
    source = ancestors // local_count
    offset = ancestors % local_count
    places = jnp.arange(local_count)
    earlier = (source[:, None] == source[None, :]) & (places[None, :] < places[:, None])
    arrival_rank = jnp.sum(earlier.astype(jnp.int32), axis=1)
    slot_index = source * capacity + arrival_rank
    slot_match = jnp.arange(slot_total)[:, None] == slot_index[None, :]
    wanted = jnp.sum(jnp.where(slot_match, offset[None, :] + 1, 0), axis=1) - 1
    requests_in = lax.all_to_all(
        wanted.reshape(devices, capacity), "dp", split_axis=0, concat_axis=0, tiled=True
    )
    picked = jnp.clip(requests_in, 0, local_count - 1).reshape(-1)
    every_prior = lax.all_gather(prior_twist, "dp", axis=0, tiled=True)
    twist_before = jnp.take(every_prior, ancestors, axis=0)
    split_query = queries.reshape(step_count, local_count, kv_count, group_size, head_size)
    sent_rows = jnp.take(gen_kv, picked, axis=0).reshape((devices, capacity) + gen_kv.shape[1:])
    arrived = lax.all_to_all(sent_rows, "dp", split_axis=0, concat_axis=0, tiled=True)
    resampled = jnp.take(arrived.reshape((slot_total,) + gen_kv.shape[1:]), slot_index, axis=0)
    cache_scores = (
        jnp.einsum(
            "spcgd,pkcd->spcgk", split_query, resampled[:, 0], preferred_element_type=jnp.float32
        )
        * scaling
    )
    largest, totals, weighted = block_state(cache_scores, resampled[:, 1], "spcgk,pkcd->spcgd")
    cached = (
        largest.reshape(step_count, local_count, head_count),
        totals.reshape(step_count, local_count, head_count),
        weighted.reshape(step_count, local_count, head_count, head_size),
    )
    new_scores = (
        jnp.einsum(
            "spcgd,tpcd->spcgt", split_query, new_kv[:, 0], preferred_element_type=jnp.float32
        )
        * scaling
    )
    positions = jnp.arange(step_count)
    allowed = positions[None, :] <= positions[:, None]
    new_scores = jnp.where(allowed[:, None, None, None, :], new_scores, -jnp.inf)
    largest, totals, weighted = block_state(new_scores, new_kv[:, 1], "spcgt,tpcd->spcgd")
    fresh_state = (
        largest.reshape(step_count, local_count, head_count),
        totals.reshape(step_count, local_count, head_count),
        weighted.reshape(step_count, local_count, head_count, head_size),
    )
    everyone = lax.all_gather(queries, "dp", axis=1, tiled=True)
    largest, totals, weighted = prompt_states(
        everyone.reshape(step_count * devices * local_count, head_count, head_size),
        prompt_kv,
        kv_count,
        scaling,
    )
    arrived_states = (
        lax.all_to_all(
            largest.reshape(step_count, devices, local_count, head_count),
            "dp",
            split_axis=1,
            concat_axis=1,
            tiled=True,
        ),
        lax.all_to_all(
            totals.reshape(step_count, devices, local_count, head_count),
            "dp",
            split_axis=1,
            concat_axis=1,
            tiled=True,
        ),
        lax.all_to_all(
            weighted.reshape(step_count, devices, local_count, head_count, head_size),
            "dp",
            split_axis=1,
            concat_axis=1,
            tiled=True,
        ),
    )
    prompt_state = fold_blocks(arrived_states[0], arrived_states[1], arrived_states[2], 1)
    joined = join_states(join_states(prompt_state, cached), fresh_state)
    attended = (joined[2] / joined[1][..., None]).astype(jnp.bfloat16)
    last_step = lax.optimization_barrier(attended[-1]).astype(jnp.float32)
    local_twist = jnp.sum(last_step * twist_vec, axis=(1, 2))
    twist_value = lax.psum(local_twist, "tensor")
    raw_weight = twist_value - twist_before
    largest_weight = lax.pmax(jnp.max(raw_weight), "dp")
    weight_mass = lax.psum(jnp.sum(jnp.exp(raw_weight - largest_weight)), "dp")
    normalizer = largest_weight + jnp.log(weight_mass)
    return (attended, raw_weight - normalizer)


def solution(mesh):
    placed = (
        P(None, ("parts", "dp"), "tensor", None),
        P(("parts", "dp"), None, None, "tensor", None),
        P(None, ("parts", "dp"), "tensor", None),
        P(None, None, ("parts", "dp"), "tensor", None),
        P(("parts", "dp")),
        P(("parts", "dp")),
        P("tensor", None),
    )
    return jax.shard_map(
        per_device,
        mesh=mesh,
        in_specs=placed,
        out_specs=(P(None, ("parts", "dp"), "tensor", None), P(("parts", "dp"))),
        check_vma=False,
    )
```

profile of v0, /device:TPU:0, one launch (start us, length us, event | category | flops | bytes accessed | tf_op | source)
XLA Modules:
  0.0 157.3 jit_solution(7130623179860953342)
XLA Ops:
  0.6 0.8 compare_select_fusion.3
  1.7 0.7 sub.106
  2.4 6.3 %all-to-all-start.2 = ((s32[4,1,4]{2,1,0:T(1,128)}), s32[4,1,4]{2,1,0:T(1,128)S(1)}, u32[]{:S(2)}, u32[]{:S(2)}) async-start(s32[4,1,4]{2,1,0:T(1,128)} %bitcast.10), calls=%async_computation.2 | async-start | bytes 4096 | tf_op jit(solution)/shard_map/all_to_all | solution.py:77
  8.7 14.6 %all_gather.6 = bf16[2,32,16,128]{3,2,1,0:T(8,128)(2,1)S(1)} all-gather(bf16[2,8,16,128]{3,2,1,0:T(8,128)(2,1)} %param.9), channel_id=1, replica_groups=mesh['parts'=2,'dp'=4,'tensor'=4] {'dp'}, dimensions={1}, use_global_device_ids=true | all-gather | bytes 327680 | tf_op jit(solution)/shard_map/all_gather | solution.py:114
  23.4 2.5 %fusion.38 = (bf16[1,1792,2,128]{3,2,1,0:T(2,128)(2,1)S(1)}, bf16[1,1792,2,128]{3,2,1,0:T(2,128)(2,1)S(1)}) fusion(bf16[2,1792,2,128]{3,2,1,0:T(2,128)(2,1)} %param.7), kind=kLoop, calls=%fused_computation.88 | loop fusion | bytes 3670016 | tf_op jit(solution)/shard_map/slice | solution.py:44
  25.9 4.1 %bitcast_reduce_fusion = (f32[64,2,8]{0,2,1:T(8,128)S(1)}, f32[2,1792,64,8]{1,2,3,0:T(8,128)}) fusion(bf16[64,2,8,128]{3,0,2,1:T(8,128)(2,1)S(1)} %bitcast.113, bf16[1,1792,2,128]{3,2,1,0:T(2,128)(2,1)S(1)} %get-tuple-element.35), kind=kOutput, calls=%fused_computation.4 | convolution fusion | flops 473431040 | bytes 8523776 | tf_op jit(solution)/shard_map/while/body/eval_jaxpr/pcgd,kcd->pcgk/dot_general | solution.py:48
  30.2 4.4 %fusion.3 = f32[2,64,8,128]{3,1,2,0:T(8,128)S(1)} fusion(f32[2,1792,64,8]{1,2,3,0:T(8,128)} %get-tuple-element.48, f32[64,2,8]{0,2,1:T(8,128)S(1)} %get-tuple-element.47, bf16[1,1792,2,128]{3,2,1,0:T(2,128)(2,1)S(1)} %get-tuple-element.34), kind=kOutput, calls=%fused_computation.8 | convolution fusion | flops 475267072 | bytes 8785920 | tf_op jit(solution)/shard_map/while/body/eval_jaxpr/pcgk,kcd->pcgd/dot_general | solution.py:32
  34.6 0.7 reshape.241
  35.3 4.9 %all-to-all-start.1 = ((f32[4,1,256]{2,1,0:T(1,128)}), f32[4,1,256]{2,1,0:T(1,128)S(1)}, u32[]{:S(2)}, u32[]{:S(2)}) async-start(f32[4,1,256]{2,1,0:T(1,128)} %reshape.241), calls=%async_computation.1 | async-start | bytes 8192 | tf_op jit(solution)/shard_map/all_to_all | solution.py:122
  40.2 4.4 %fusion.1 = f32[64,2,8]{0,2,1:T(8,128)S(1)} fusion(f32[2,1792,64,8]{1,2,3,0:T(8,128)} %get-tuple-element.48, f32[64,2,8]{0,2,1:T(8,128)S(1)} %get-tuple-element.47), kind=kLoop, calls=%fused_computation.6 | loop fusion | flops 5504000 | bytes 7348224 | tf_op jit(solution)/shard_map/while/body/eval_jaxpr/reduce_sum | solution.py:35
  44.6 1.1 copy.104
  45.9 0.7 reshape.243
  46.6 5.1 %all-to-all-start.4 = ((f32[4,1,256]{2,1,0:T(1,128)}), f32[4,1,256]{2,1,0:T(1,128)S(1)}, u32[]{:S(2)}, u32[]{:S(2)}) async-start(f32[4,1,256]{2,1,0:T(1,128)} %reshape.243), calls=%async_computation.4 | async-start | bytes 8192 | tf_op jit(solution)/shard_map/all_to_all | solution.py:129
  51.8 5.5 %all-to-all-done.4 = f32[4,1,256]{2,1,0:T(1,128)S(1)} async-done(((f32[4,1,256]{2,1,0:T(1,128)}), f32[4,1,256]{2,1,0:T(1,128)S(1)}, u32[]{:S(2)}, u32[]{:S(2)}) %all-to-all-start.4) | async-done | bytes 4128 | tf_op jit(solution)/shard_map/all_to_all | solution.py:129
  57.3 4.1 %all-to-all-start = ((f32[2,4,8,16,128]{4,3,2,0,1:T(8,128)}), f32[2,4,8,16,128]{4,3,2,0,1:T(8,128)}, u32[]{:S(2)}, u32[]{:S(2)}) async-start(f32[2,4,8,16,128]{4,3,2,0,1:T(8,128)} %copy.104), calls=%async_computation | async-start | bytes 1048576 | tf_op jit(solution)/shard_map/all_to_all | solution.py:136
  61.4 5.1 %gather_fusion = bf16[16,2,128,2,128]{4,3,2,1,0:T(2,128)(2,1)S(1)} fusion(bf16[8,2,128,2,128]{4,3,2,1,0:T(2,128)(2,1)S(1)} %copy-done, s32[1024]{0:T(1024)S(1)} %pad_clamp_fusion.2), kind=kCustom, calls=%fused_computation | custom fusion | bytes 4194368 | tf_op jit(solution)/shard_map/jit(_take)/gather | solution.py:84
  66.5 1.7 %copy_select_fusion = bf16[4,4,2,128,2,128]{5,3,4,2,1,0:T(8,128)(2,1)} fusion(bf16[4,4,2,128,2,128]{5,4,3,2,1,0:T(2,128)(2,1)S(1)} %bitcast.110, pred[4,4]{1,0:T(4,128)(4,1)S(1)} %compare_and_fusion), kind=kLoop, calls=%fused_computation.11 | loop fusion | flops 1048576 | bytes 4194320 | tf_op jit(solution)/shard_map/jit(_take)/select_n | solution.py:84
  68.2 3.6 %all-to-all-done = f32[2,4,8,16,128]{4,3,2,0,1:T(8,128)} async-done(((f32[2,4,8,16,128]{4,3,2,0,1:T(8,128)}), f32[2,4,8,16,128]{4,3,2,0,1:T(8,128)}, u32[]{:S(2)}, u32[]{:S(2)}) %all-to-all-start) | async-done | bytes 524320 | tf_op jit(solution)/shard_map/all_to_all | solution.py:136
  71.9 3.6 %all-to-all-start.3 = ((bf16[4,4,2,128,2,128]{5,3,4,2,1,0:T(8,128)(2,1)}), bf16[4,4,2,128,2,128]{5,3,4,2,1,0:T(8,128)(2,1)S(1)}, u32[]{:S(2)}, u32[]{:S(2)}) async-start(bf16[4,4,2,128,2,128]{5,3,4,2,1,0:T(8,128)(2,1)} %copy_select_fusion), calls=%async_computation.3 | async-start | bytes 4194304 | tf_op jit(solution)/shard_map/all_to_all | solution.py:85
  77.7 31.2 %all-reduce = f32[32]{0:T(128)S(1)} all-reduce(f32[32]{0:T(128)S(1)} %dynamic-update-slice), channel_id=1, replica_groups=mesh['parts'=2,'dp'=4,'tensor'=4] {'dp'}, use_global_device_ids=true, to_apply=%add | all-reduce | flops 32 | bytes 256
  109.7 0.7 reduce.4
  110.4 0.7 reduce.5
  111.2 1.3 multiply_reduce_fusion
  112.5 4.7 %all-to-all-done.3 = bf16[4,4,2,128,2,128]{5,3,4,2,1,0:T(8,128)(2,1)S(1)} async-done(((bf16[4,4,2,128,2,128]{5,3,4,2,1,0:T(8,128)(2,1)}), bf16[4,4,2,128,2,128]{5,3,4,2,1,0:T(8,128)(2,1)S(1)}, u32[]{:S(2)}, u32[]{:S(2)}) %all-to-all-start.3) | async-done | bytes 2097184 | tf_op jit(solution)/shard_map/all_to_all | solution.py:85
  117.2 1.7 %gather_fusion.1 = bf16[8,2,128,2,128]{4,2,3,1,0:T(8,128)(2,1)} fusion(bf16[16,2,128,2,128]{4,2,3,1,0:T(8,128)(2,1)S(1)} %bitcast.111, s32[1024]{0:T(1024)S(1)} %pad_clamp_fusion.1), kind=kCustom, calls=%fused_computation.1 | custom fusion | bytes 2097184 | tf_op jit(solution)/shard_map/jit(_take)/gather | solution.py:86
  118.9 1.4 copy_select_fusion.1
  121.9 0.6 gather_fusion.2
  122.6 5.7 %psum.14 = f32[8]{0:T(128)S(1)} all-reduce(f32[8]{0:T(128)S(1)} %multiply_reduce_fusion.1), channel_id=1, replica_groups=mesh['parts'=2,'dp'=4,'tensor'=4] {'tensor'}, use_global_device_ids=true, to_apply=%region_12.13 | all-reduce | flops 8 | bytes 64 | tf_op jit(solution)/shard_map/psum | solution.py:149
  128.2 0.6 fusion.34
  128.8 16.2 %pmax.7 = f32[]{:T(128)} all-reduce(f32[]{:T(128)} %get-tuple-element.16), channel_id=1, replica_groups=mesh['parts'=2,'dp'=4,'tensor'=4] {'dp'}, use_global_device_ids=true, to_apply=%region_14.15 | all-reduce | flops 1 | bytes 8 | tf_op jit(solution)/shard_map/pmax | solution.py:151
  145.0 1.3 exponential_reduce_fusion
  146.3 9.1 %psum.15 = f32[]{:T(128)} all-reduce(f32[]{:T(128)} %exponential_reduce_fusion), channel_id=1, replica_groups=mesh['parts'=2,'dp'=4,'tensor'=4] {'dp'}, use_global_device_ids=true, to_apply=%region_16.17 | all-reduce | flops 1 | bytes 8 | tf_op jit(solution)/shard_map/psum | solution.py:152
  (64 shorter events, 5.5 us)
Async XLA Ops:
  0.6 60.8 %copy-start = (bf16[8,2,128,2,128]{4,3,2,1,0:T(2,128)(2,1)S(1)}, bf16[8,2,128,2,128]{4,3,2,1,0:T(2,128)(2,1)}, u32[]{:S(2)}) copy-start(bf16[8,2,128,2,128]{4,3,2,1,0:T(2,128)(2,1)} %param.8) | copy-start | bytes 3145732
  2.4 32.9 %all-to-all-start.2 = ((s32[4,1,4]{2,1,0:T(1,128)}), s32[4,1,4]{2,1,0:T(1,128)S(1)}, u32[]{:S(2)}, u32[]{:S(2)}) async-start(s32[4,1,4]{2,1,0:T(1,128)} %bitcast.10), calls=%async_computation.2 | async-start | bytes 4096 | tf_op jit(solution)/shard_map/all_to_all | solution.py:77
  35.3 11.3 %all-to-all-start.1 = ((f32[4,1,256]{2,1,0:T(1,128)}), f32[4,1,256]{2,1,0:T(1,128)S(1)}, u32[]{:S(2)}, u32[]{:S(2)}) async-start(f32[4,1,256]{2,1,0:T(1,128)} %reshape.241), calls=%async_computation.1 | async-start | bytes 8192 | tf_op jit(solution)/shard_map/all_to_all | solution.py:122
  44.6 30.9 %copy-start.3 = (bf16[2,2,8,2,128]{4,3,2,1,0:T(2,128)(2,1)S(1)}, bf16[2,2,8,2,128]{4,3,2,1,0:T(2,128)(2,1)}, u32[]{:S(2)}) copy-start(bf16[2,2,8,2,128]{4,3,2,1,0:T(2,128)(2,1)} %param.10) | copy-start | bytes 49156
  44.6 30.9 %copy-start.2 = (bf16[2,8,16,128]{3,2,1,0:T(8,128)(2,1)S(1)}, bf16[2,8,16,128]{3,2,1,0:T(8,128)(2,1)}, u32[]{:S(2)}) copy-start(bf16[2,8,16,128]{3,2,1,0:T(8,128)(2,1)} %param.9) | copy-start | bytes 196612
  45.7 30.5 %copy-start.7 = (u32[32]{0:T(128)S(1)}, u32[32]{0:T(128)}, u32[]{:S(2)}) copy-start(u32[32]{0:T(128)} %constant.108) | copy-start | bytes 388
  45.7 31.8 %copy-start.6 = (f32[8]{0:T(128)S(1)}, f32[8]{0:T(128)}, u32[]{:S(2)}) copy-start(f32[8]{0:T(128)} %param.12) | copy-start | bytes 100
  46.6 10.7 %all-to-all-start.4 = ((f32[4,1,256]{2,1,0:T(1,128)}), f32[4,1,256]{2,1,0:T(1,128)S(1)}, u32[]{:S(2)}, u32[]{:S(2)}) async-start(f32[4,1,256]{2,1,0:T(1,128)} %reshape.243), calls=%async_computation.4 | async-start | bytes 8192 | tf_op jit(solution)/shard_map/all_to_all | solution.py:129
  57.3 14.6 %all-to-all-start = ((f32[2,4,8,16,128]{4,3,2,0,1:T(8,128)}), f32[2,4,8,16,128]{4,3,2,0,1:T(8,128)}, u32[]{:S(2)}, u32[]{:S(2)}) async-start(f32[2,4,8,16,128]{4,3,2,0,1:T(8,128)} %copy.104), calls=%async_computation | async-start | bytes 1048576 | tf_op jit(solution)/shard_map/all_to_all | solution.py:136
  68.2 53.6 %copy-start.4 = (f32[16,128]{1,0:T(8,128)S(1)}, f32[16,128]{1,0:T(8,128)}, u32[]{:S(2)}) copy-start(f32[16,128]{1,0:T(8,128)} %param.13) | copy-start | bytes 24580
  68.2 60.0 %copy-start.5 = (s32[8]{0:T(128)S(1)}, s32[8]{0:T(128)}, u32[]{:S(2)}) copy-start(s32[8]{0:T(128)} %param.11) | copy-start | bytes 100
  71.9 45.4 %all-to-all-start.3 = ((bf16[4,4,2,128,2,128]{5,3,4,2,1,0:T(8,128)(2,1)}), bf16[4,4,2,128,2,128]{5,3,4,2,1,0:T(8,128)(2,1)S(1)}, u32[]{:S(2)}, u32[]{:S(2)}) async-start(bf16[4,4,2,128,2,128]{5,3,4,2,1,0:T(8,128)(2,1)} %copy_select_fusion), calls=%async_computation.3 | async-start | bytes 4194304 | tf_op jit(solution)/shard_map/all_to_all | solution.py:85
  121.8 35.5 %copy-start.1 = (bf16[2,8,16,128]{3,2,1,0:T(8,128)(2,1)}, bf16[2,8,16,128]{3,2,1,0:T(8,128)(2,1)S(1)}, u32[]{:S(2)}) copy-start(bf16[2,8,16,128]{3,2,1,0:T(8,128)(2,1)S(1)} %fusion.13) | copy-start | bytes 196612
where the time goes:
time: 158 us; the launch traced here: 157 us
  blocking collectives  76.7 us (49%)
  starting transfers between devices  24 us (15%)
  local copies, waits for them, and re-layouts  15.5 us (10%)
  other arithmetic  14.3 us (9%)
  waiting for transfers between devices  13.8 us (9%)
  matrix products  9.94 us (6%)
  between operations  2.94 us (2%)
    unnamed x1, blocking collectives  31.2 us
    pmax x1, blocking collectives, per_device(): largest_weight = lax.pmax(jnp.max(raw_weight), 'dp')  16.2 us
    all_gather x1, blocking collectives, per_device(): everyone = lax.all_gather(queries, 'dp', axis=1, tiled=True)  14.6 us
    psum x1, blocking collectives, per_device(): weight_mass = lax.psum(jnp.sum(jnp.exp(raw_weight - largest_weight)), 'dp')  9.05 us
    all_to_all x1, starting transfers between devices, per_device(): lax.all_to_all(wanted.reshape(devices, capacity), 'dp', split_axis=0, con...  6.35 us
    psum x1, blocking collectives, per_device(): twist_value = lax.psum(local_twist, 'tensor')  5.66 us
    all_to_all x1, waiting for transfers between devices, per_device(): lax.all_to_all(totals.reshape(step_count, devices, local_count, head_coun...  5.47 us
    all_to_all x1, starting transfers between devices, per_device(): lax.all_to_all(totals.reshape(step_count, devices, local_count, head_coun...  5.09 us
  transfers between devices with their start and end apart: 5, of which 3 were waited for; matrix products, arithmetic and copies ran while one was open for 19% of the time, Pallas kernels for 0%

commit v1 on v0

--- a/solution.py
+++ b/solution.py
@@ -111,7 +111,19 @@
         totals.reshape(step_count, local_count, head_count),
         weighted.reshape(step_count, local_count, head_count, head_size),
     )
-    everyone = lax.all_gather(queries, "dp", axis=1, tiled=True)
+    chips = lax.axis_size("dp")
+    pile = [(to_i, (to_i + 1) % chips) for to_i in range(chips)]
+    copies = [(to_i, (to_i - 1) % chips) for to_i in range(chips)]
+    near, big = ([queries], [queries])
+    for _ in range(chips // 2):
+        near.append(lax.ppermute(near[-1], "dp", perm=pile))
+    for _ in range((chips - 1) // 2):
+        big.append(lax.ppermute(big[-1], "dp", copies))
+    everyone = jnp.roll(
+        jnp.concatenate([*near[::-1], *big[1:]], axis=1),
+        shift=(lax.axis_index("dp") - chips // 2) * queries.shape[1],
+        axis=1,
+    )
     largest, totals, weighted = prompt_states(
         everyone.reshape(step_count * devices * local_count, head_count, head_size),
         prompt_kv,

time: 158 us -> 151 us (0.956)
  blocking collectives: 76.7 us -> 65.9 us
  local copies, waits for them, and re-layouts: 15.5 us -> 20.1 us
  other arithmetic: 14.3 us -> 11.2 us
  starting transfers between devices: 24 us -> 27.1 us
  matrix products: 9.94 us -> 6.93 us
  waiting for transfers between devices: 13.8 us -> 15.6 us
    all_gather x1 -> x0, blocking collectives: 14.6 us -> none  [per_device(): everyone = lax.all_gather(queries, 'dp', axis=1, tiled=True)]
    ppermute x0 -> x3, starting transfers between devices: none -> 7.16 us  [the longest x1 5.13 us: per_device(): big.append(lax.ppermute(big[-1], 'dp', copies))]
    unnamed x23 -> x32, local copies, waits for them, and re-layouts: 2.39 us -> 7.14 us
    unnamed x1, blocking collectives: 31.2 us -> 35 us
    reduce_sum x3, other arithmetic: 4.73 us -> 1.64 us  [block_state(): return (largest, jnp.sum(exponent, axis=-1), weighted)]
    dot_general x1, matrix products: 4.1 us -> 1.2 us  [attend_block(): jnp.einsum('pcgd,kcd->pcgk', query_block, key_rows, preferred_element_typ...]
    all_to_all x1, starting transfers between devices: 5.09 us -> 3.25 us  [per_device(): lax.all_to_all(totals.reshape(step_count, devices, local_count, head_coun...]
    ppermute x0 -> x3, waiting for transfers between devices: none -> 1.7 us  [the longest x2 1.7 us: per_device(): near.append(lax.ppermute(near[-1], 'dp', perm=pile))]
  transfers between devices with their start and end apart: 5 -> 8, of which waited for: 3 -> 5; matrix products, arithmetic and copies ran while one was open for 19% -> 18% of each run, Pallas kernels for 0% -> 0%
where the time goes in v1:
time: 151 us; the launch traced here: 150 us
  blocking collectives  65.9 us (44%)
  starting transfers between devices  27.1 us (18%)
  local copies, waits for them, and re-layouts  20.1 us (13%)
  waiting for transfers between devices  15.6 us (10%)
  other arithmetic  11.2 us (7%)
  matrix products  6.93 us (5%)
  between operations  3.03 us (2%)
    unnamed x1, blocking collectives  35 us
    pmax x1, blocking collectives, per_device(): largest_weight = lax.pmax(jnp.max(raw_weight), 'dp')  16 us
    psum x1, blocking collectives, per_device(): weight_mass = lax.psum(jnp.sum(jnp.exp(raw_weight - largest_weight)), 'dp')  9.05 us
    unnamed x32, local copies, waits for them, and re-layouts  7.14 us
    psum x1, blocking collectives, per_device(): twist_value = lax.psum(local_twist, 'tensor')  5.82 us
    ppermute x1, starting transfers between devices, per_device(): big.append(lax.ppermute(big[-1], 'dp', copies))  5.13 us
    all_to_all x1, starting transfers between devices, per_device(): lax.all_to_all(wanted.reshape(devices, capacity), 'dp', split_axis=0, con...  5.09 us
    gather x1, local copies, waits for them, and re-layouts, per_device(): jnp.take(gen_kv, picked, axis=0)  5.09 us
  transfers between devices with their start and end apart: 8, of which 5 were waited for; matrix products, arithmetic and copies ran while one was open for 18% of the time, Pallas kernels for 0%

profile of v1, /device:TPU:0, one launch (start us, length us, event | category | flops | bytes accessed | tf_op | source)
XLA Modules:
  0.0 149.9 jit_solution(12539336047507572728)
XLA Ops:
  0.6 5.1 %collective-permute-start.2 = (bf16[2,8,16,128]{3,2,1,0:T(8,128)(2,1)}, bf16[2,8,16,128]{3,2,1,0:T(8,128)(2,1)S(1)}, u32[]{:S(2)}, u32[]{:S(2)}) collective-permute-start(bf16[2,8,16,128]{3,2,1,0:T(8,128)(2,1)} %param.9), channel_id=1, source_target_pairs={{0,12},{4,0},{8,4},{12,8},{1,13},{5,1},{9,5},{13,9},{2,14},{6,2},{... | collective-permute-start | bytes 196616 | tf_op jit(solution)/shard_map/ppermute | solution.py:121
  7.4 5.1 %all-to-all-start.2 = ((s32[4,1,4]{2,1,0:T(1,128)}), s32[4,1,4]{2,1,0:T(1,128)S(1)}, u32[]{:S(2)}, u32[]{:S(2)}) async-start(s32[4,1,4]{2,1,0:T(1,128)} %bitcast.10), calls=%async_computation.2 | async-start | bytes 4096 | tf_op jit(solution)/shard_map/all_to_all | solution.py:77
  12.5 2.0 %collective-permute-start.1 = (bf16[2,8,16,128]{3,2,1,0:T(8,128)(2,1)S(1)}, bf16[2,8,16,128]{3,2,1,0:T(8,128)(2,1)S(1)}, u32[]{:S(2)}, u32[]{:S(2)}) collective-permute-start(bf16[2,8,16,128]{3,2,1,0:T(8,128)(2,1)S(1)} %collective-permute-done), channel_id=1, source_target_pairs={{0,4},{4,8},{8,12},{12,0},{1,5},{5,9},{9,13},{13,1},{2,6},{6,10},{... | collective-permute-start | bytes 196616 | tf_op jit(solution)/shard_map/ppermute | solution.py:119
  14.5 2.5 %fusion.42 = (bf16[1,1792,2,128]{3,2,1,0:T(2,128)(2,1)S(1)}, bf16[1,1792,2,128]{3,2,1,0:T(2,128)(2,1)S(1)}) fusion(bf16[2,1792,2,128]{3,2,1,0:T(2,128)(2,1)} %param.7), kind=kLoop, calls=%fused_computation.99 | loop fusion | bytes 3670016 | tf_op jit(solution)/shard_map/slice | solution.py:44
  17.0 1.7 %collective-permute-done.1 = bf16[2,8,16,128]{3,2,1,0:T(8,128)(2,1)S(1)} collective-permute-done((bf16[2,8,16,128]{3,2,1,0:T(8,128)(2,1)S(1)}, bf16[2,8,16,128]{3,2,1,0:T(8,128)(2,1)S(1)}, u32[]{:S(2)}, u32[]{:S(2)}) %collective-permute-start.1) | collective-permute-done | bytes 65568 | tf_op jit(solution)/shard_map/ppermute | solution.py:119
  18.7 0.9 constant_dynamic-update-slice_fusion.5
  19.6 0.9 constant_dynamic-update-slice_fusion.1
  20.6 1.2 bitcast_reduce_fusion
  21.8 3.0 %copy-done.1 = f32[2,64,8,1792]{3,2,1,0:T(8,128)} copy-done((f32[2,64,8,1792]{3,2,1,0:T(8,128)}, f32[2,64,8,1792]{3,2,1,0:T(8,128)S(1)}, u32[]{:S(2)}) %copy-start.1) | copy-done | bytes 7340056
  24.7 1.3 fusion.1
  26.3 0.7 reshape.243
  27.0 3.2 %all-to-all-start.4 = ((f32[4,1,256]{2,1,0:T(1,128)}), f32[4,1,256]{2,1,0:T(1,128)S(1)}, u32[]{:S(2)}, u32[]{:S(2)}) async-start(f32[4,1,256]{2,1,0:T(1,128)} %reshape.243), calls=%async_computation.4 | async-start | bytes 8192 | tf_op jit(solution)/shard_map/all_to_all | solution.py:141
  30.6 0.7 reshape.241
  31.3 4.3 %all-to-all-done.4 = f32[4,1,256]{2,1,0:T(1,128)S(1)} async-done(((f32[4,1,256]{2,1,0:T(1,128)}), f32[4,1,256]{2,1,0:T(1,128)S(1)}, u32[]{:S(2)}, u32[]{:S(2)}) %all-to-all-start.4) | async-done | bytes 4128 | tf_op jit(solution)/shard_map/all_to_all | solution.py:141
  35.7 3.2 %all-to-all-start.1 = ((f32[4,1,256]{2,1,0:T(1,128)}), f32[4,1,256]{2,1,0:T(1,128)S(1)}, u32[]{:S(2)}, u32[]{:S(2)}) async-start(f32[4,1,256]{2,1,0:T(1,128)} %reshape.241), calls=%async_computation.1 | async-start | bytes 8192 | tf_op jit(solution)/shard_map/all_to_all | solution.py:134
  38.9 4.3 %fusion.7 = f32[64,2,8,128]{3,2,0,1:T(8,128)S(1)} fusion(f32[2,64,8,1792]{3,2,1,0:T(8,128)} %copy-done.1, f32[64,2,8]{2,0,1:T(8,128)S(1)} %get-tuple-element.47, bf16[1,1792,2,128]{3,2,1,0:T(2,128)(2,1)S(1)} %get-tuple-element.34), kind=kOutput, calls=%fused_computation.12 | convolution fusion | flops 475267072 | bytes 8785920 | tf_op jit(solution)/shard_map/while/body/eval_jaxpr/pcgk,kcd->pcgd/dot_general | solution.py:32
  43.3 0.8 copy.104
  44.5 4.8 %all-to-all-start = ((f32[2,4,8,16,128]{4,3,2,0,1:T(8,128)}), f32[2,4,8,16,128]{4,3,2,0,1:T(8,128)}, u32[]{:S(2)}, u32[]{:S(2)}) async-start(f32[2,4,8,16,128]{4,3,2,0,1:T(8,128)} %copy.104), calls=%async_computation | async-start | bytes 1048576 | tf_op jit(solution)/shard_map/all_to_all | solution.py:148
  49.3 5.1 %gather_fusion = bf16[16,2,128,2,128]{4,3,2,1,0:T(2,128)(2,1)S(1)} fusion(bf16[8,2,128,2,128]{4,3,2,1,0:T(2,128)(2,1)S(1)} %copy-done, s32[1024]{0:T(1024)S(1)} %pad_clamp_fusion.2), kind=kCustom, calls=%fused_computation | custom fusion | bytes 4194368 | tf_op jit(solution)/shard_map/jit(_take)/gather | solution.py:84
  54.4 1.7 %copy_select_fusion = bf16[4,4,2,128,2,128]{5,3,4,2,1,0:T(8,128)(2,1)} fusion(bf16[4,4,2,128,2,128]{5,4,3,2,1,0:T(2,128)(2,1)S(1)} %bitcast.111, pred[4,4]{1,0:T(4,128)(4,1)S(1)} %compare_and_fusion), kind=kLoop, calls=%fused_computation.11 | loop fusion | flops 1048576 | bytes 4194320 | tf_op jit(solution)/shard_map/jit(_take)/select_n | solution.py:84
  56.0 4.5 %all-to-all-done = f32[2,4,8,16,128]{4,3,2,0,1:T(8,128)} async-done(((f32[2,4,8,16,128]{4,3,2,0,1:T(8,128)}), f32[2,4,8,16,128]{4,3,2,0,1:T(8,128)}, u32[]{:S(2)}, u32[]{:S(2)}) %all-to-all-start) | async-done | bytes 524320 | tf_op jit(solution)/shard_map/all_to_all | solution.py:148
  60.6 3.6 %all-to-all-start.3 = ((bf16[4,4,2,128,2,128]{5,3,4,2,1,0:T(8,128)(2,1)}), bf16[4,4,2,128,2,128]{5,3,4,2,1,0:T(8,128)(2,1)S(1)}, u32[]{:S(2)}, u32[]{:S(2)}) async-start(bf16[4,4,2,128,2,128]{5,3,4,2,1,0:T(8,128)(2,1)} %copy_select_fusion), calls=%async_computation.3 | async-start | bytes 4194304 | tf_op jit(solution)/shard_map/all_to_all | solution.py:85
  66.4 35.0 %all-reduce = f32[32]{0:T(128)S(1)} all-reduce(f32[32]{0:T(128)S(1)} %dynamic-update-slice), channel_id=1, replica_groups=mesh['parts'=2,'dp'=4,'tensor'=4] {'dp'}, use_global_device_ids=true, to_apply=%add | all-reduce | flops 32 | bytes 256
  103.0 0.7 reduce.4
  103.8 1.3 multiply_reduce_fusion
  105.1 4.8 %all-to-all-done.3 = bf16[4,4,2,128,2,128]{5,3,4,2,1,0:T(8,128)(2,1)S(1)} async-done(((bf16[4,4,2,128,2,128]{5,3,4,2,1,0:T(8,128)(2,1)}), bf16[4,4,2,128,2,128]{5,3,4,2,1,0:T(8,128)(2,1)S(1)}, u32[]{:S(2)}, u32[]{:S(2)}) %all-to-all-start.3) | async-done | bytes 2097184 | tf_op jit(solution)/shard_map/all_to_all | solution.py:85
  109.8 1.7 %gather_fusion.1 = bf16[8,2,128,2,128]{4,2,3,1,0:T(8,128)(2,1)} fusion(bf16[16,2,128,2,128]{4,2,3,1,0:T(8,128)(2,1)S(1)} %bitcast.112, s32[1024]{0:T(1024)S(1)} %pad_clamp_fusion.1), kind=kCustom, calls=%fused_computation.1 | custom fusion | bytes 2097184 | tf_op jit(solution)/shard_map/jit(_take)/gather | solution.py:86
  111.5 1.4 copy_select_fusion.1
  115.2 5.8 %psum.14 = f32[8]{0:T(128)S(1)} all-reduce(f32[8]{0:T(128)S(1)} %multiply_reduce_fusion.1), channel_id=1, replica_groups=mesh['parts'=2,'dp'=4,'tensor'=4] {'tensor'}, use_global_device_ids=true, to_apply=%region_12.13 | all-reduce | flops 8 | bytes 64 | tf_op jit(solution)/shard_map/psum | solution.py:161
  121.6 16.0 %pmax.7 = f32[]{:T(128)} all-reduce(f32[]{:T(128)} %get-tuple-element.16), channel_id=1, replica_groups=mesh['parts'=2,'dp'=4,'tensor'=4] {'dp'}, use_global_device_ids=true, to_apply=%region_14.15 | all-reduce | flops 1 | bytes 8 | tf_op jit(solution)/shard_map/pmax | solution.py:163
  137.6 1.3 exponential_reduce_fusion
  138.9 9.1 %psum.15 = f32[]{:T(128)} all-reduce(f32[]{:T(128)} %exponential_reduce_fusion), channel_id=1, replica_groups=mesh['parts'=2,'dp'=4,'tensor'=4] {'dp'}, use_global_device_ids=true, to_apply=%region_16.17 | all-reduce | flops 1 | bytes 8 | tf_op jit(solution)/shard_map/psum | solution.py:164
  (82 shorter events, 9.2 us)
Async XLA Ops:
  0.6 48.6 %copy-start = (bf16[8,2,128,2,128]{4,3,2,1,0:T(2,128)(2,1)S(1)}, bf16[8,2,128,2,128]{4,3,2,1,0:T(2,128)(2,1)}, u32[]{:S(2)}) copy-start(bf16[8,2,128,2,128]{4,3,2,1,0:T(2,128)(2,1)} %param.8) | copy-start | bytes 3145732
  0.6 18.9 %collective-permute-start.2 = (bf16[2,8,16,128]{3,2,1,0:T(8,128)(2,1)}, bf16[2,8,16,128]{3,2,1,0:T(8,128)(2,1)S(1)}, u32[]{:S(2)}, u32[]{:S(2)}) collective-permute-start(bf16[2,8,16,128]{3,2,1,0:T(8,128)(2,1)} %param.9), channel_id=1, source_target_pairs={{0,12},{4,0},{8,4},{12,8},{1,13},{5,1},{9,5},{13,9},{2,14},{6,2},{... | collective-permute-start | bytes 196616 | tf_op jit(solution)/shard_map/ppermute | solution.py:121
  5.8 6.7 %collective-permute-start = (bf16[2,8,16,128]{3,2,1,0:T(8,128)(2,1)}, bf16[2,8,16,128]{3,2,1,0:T(8,128)(2,1)S(1)}, u32[]{:S(2)}, u32[]{:S(2)}) collective-permute-start(bf16[2,8,16,128]{3,2,1,0:T(8,128)(2,1)} %param.9), channel_id=1, source_target_pairs={{0,4},{4,8},{8,12},{12,0},{1,5},{5,9},{9,13},{13,1},{2,6},{6,10},{... | collective-permute-start | bytes 196616 | tf_op jit(solution)/shard_map/ppermute | solution.py:119
  7.4 19.6 %all-to-all-start.2 = ((s32[4,1,4]{2,1,0:T(1,128)}), s32[4,1,4]{2,1,0:T(1,128)S(1)}, u32[]{:S(2)}, u32[]{:S(2)}) async-start(s32[4,1,4]{2,1,0:T(1,128)} %bitcast.10), calls=%async_computation.2 | async-start | bytes 4096 | tf_op jit(solution)/shard_map/all_to_all | solution.py:77
  12.5 6.2 %collective-permute-start.1 = (bf16[2,8,16,128]{3,2,1,0:T(8,128)(2,1)S(1)}, bf16[2,8,16,128]{3,2,1,0:T(8,128)(2,1)S(1)}, u32[]{:S(2)}, u32[]{:S(2)}) collective-permute-start(bf16[2,8,16,128]{3,2,1,0:T(8,128)(2,1)S(1)} %collective-permute-done), channel_id=1, source_target_pairs={{0,4},{4,8},{8,12},{12,0},{1,5},{5,9},{9,13},{13,1},{2,6},{6,10},{... | collective-permute-start | bytes 196616 | tf_op jit(solution)/shard_map/ppermute | solution.py:119
  21.8 3.0 %copy-start.1 = (f32[2,64,8,1792]{3,2,1,0:T(8,128)}, f32[2,64,8,1792]{3,2,1,0:T(8,128)S(1)}, u32[]{:S(2)}) copy-start(f32[2,64,8,1792]{3,2,1,0:T(8,128)S(1)} %get-tuple-element.48) | copy-start | bytes 22020100
  27.0 8.6 %all-to-all-start.4 = ((f32[4,1,256]{2,1,0:T(1,128)}), f32[4,1,256]{2,1,0:T(1,128)S(1)}, u32[]{:S(2)}, u32[]{:S(2)}) async-start(f32[4,1,256]{2,1,0:T(1,128)} %reshape.243), calls=%async_computation.4 | async-start | bytes 8192 | tf_op jit(solution)/shard_map/all_to_all | solution.py:141
  35.7 8.8 %all-to-all-start.1 = ((f32[4,1,256]{2,1,0:T(1,128)}), f32[4,1,256]{2,1,0:T(1,128)S(1)}, u32[]{:S(2)}, u32[]{:S(2)}) async-start(f32[4,1,256]{2,1,0:T(1,128)} %reshape.241), calls=%async_computation.1 | async-start | bytes 8192 | tf_op jit(solution)/shard_map/all_to_all | solution.py:134
  43.3 20.9 %copy-start.4 = (bf16[2,2,8,2,128]{4,3,2,1,0:T(2,128)(2,1)S(1)}, bf16[2,2,8,2,128]{4,3,2,1,0:T(2,128)(2,1)}, u32[]{:S(2)}) copy-start(bf16[2,2,8,2,128]{4,3,2,1,0:T(2,128)(2,1)} %param.10) | copy-start | bytes 49156
  43.3 20.9 %copy-start.2 = (bf16[2,8,16,128]{3,2,1,0:T(8,128)(2,1)S(1)}, bf16[2,8,16,128]{3,2,1,0:T(8,128)(2,1)}, u32[]{:S(2)}) copy-start(bf16[2,8,16,128]{3,2,1,0:T(8,128)(2,1)} %param.9) | copy-start | bytes 196612
  43.3 21.6 %copy-start.8 = (u32[32]{0:T(128)S(1)}, u32[32]{0:T(128)}, u32[]{:S(2)}) copy-start(u32[32]{0:T(128)} %constant.135) | copy-start | bytes 388
  43.3 22.9 %copy-start.7 = (f32[8]{0:T(128)S(1)}, f32[8]{0:T(128)}, u32[]{:S(2)}) copy-start(f32[8]{0:T(128)} %param.12) | copy-start | bytes 100
  44.5 16.1 %all-to-all-start = ((f32[2,4,8,16,128]{4,3,2,0,1:T(8,128)}), f32[2,4,8,16,128]{4,3,2,0,1:T(8,128)}, u32[]{:S(2)}, u32[]{:S(2)}) async-start(f32[2,4,8,16,128]{4,3,2,0,1:T(8,128)} %copy.104), calls=%async_computation | async-start | bytes 1048576 | tf_op jit(solution)/shard_map/all_to_all | solution.py:148
  56.0 58.4 %copy-start.5 = (f32[16,128]{1,0:T(8,128)S(1)}, f32[16,128]{1,0:T(8,128)}, u32[]{:S(2)}) copy-start(f32[16,128]{1,0:T(8,128)} %param.13) | copy-start | bytes 24580
  56.0 65.0 %copy-start.6 = (s32[8]{0:T(128)S(1)}, s32[8]{0:T(128)}, u32[]{:S(2)}) copy-start(s32[8]{0:T(128)} %param.11) | copy-start | bytes 100
  60.6 49.3 %all-to-all-start.3 = ((bf16[4,4,2,128,2,128]{5,3,4,2,1,0:T(8,128)(2,1)}), bf16[4,4,2,128,2,128]{5,3,4,2,1,0:T(8,128)(2,1)S(1)}, u32[]{:S(2)}, u32[]{:S(2)}) async-start(bf16[4,4,2,128,2,128]{5,3,4,2,1,0:T(8,128)(2,1)} %copy_select_fusion), calls=%async_computation.3 | async-start | bytes 4194304 | tf_op jit(solution)/shard_map/all_to_all | solution.py:85
  114.4 35.5 %copy-start.3 = (bf16[2,8,16,128]{3,2,1,0:T(8,128)(2,1)}, bf16[2,8,16,128]{3,2,1,0:T(8,128)(2,1)S(1)}, u32[]{:S(2)}) copy-start(bf16[2,8,16,128]{3,2,1,0:T(8,128)(2,1)S(1)} %fusion.17) | copy-start | bytes 196612
